TPU v7x, 32 devices: a whole 2x2x4 slice. The times are simulated.
32 devices in a mesh: row: 16 (over z, y, x), col: 2 (over core).
Axes of the slice: x: 2, y: 2, z: 4, core: 2. Of those that a mesh axis runs over, the one named last changes fastest.
Arguments:
- panel: bfloat16 [65536, 256], P('row'), may hold values from -400 to 400, as said below
- slab: bfloat16 [65536, 1024], P('row', 'col'), may hold values from -300 to 300
Outputs:
- factor: float32 [256, 256], P(None, 'col')
- coupling: float32 [256, 1024], P(None, 'col')
- remainder: bfloat16 [65536, 1024], P('row', 'col')
Inputs may be any that keep to these rules, and one draw needn't show every extreme that they name: panel has full column rank.
All inputs are finite; a program needn't handle non-finite values.
Results may differ from a plain program's by a relative error of at most 0.015.
The roundings to bfloat16 on the way count: a program that leaves them out, or rounds other values in their place, can miss the bound.
Values sent between devices are 32-bit elements; how exact they have to be, the bound alone decides.
A program may use at most 64 MiB of HBM per device.

v0:
```python
import jax
import jax.numpy as jnp
from jax import lax
from jax.sharding import PartitionSpec as P


def matmul(left, right):
    return jnp.dot(left, right, precision=lax.Precision.HIGHEST)


def factor_inverse(gram):
    order = gram.shape[0]
    if order == 1:
        root = jnp.sqrt(gram)
        return (root, 1.0 / root)
    half = order // 2
    upper_left, upper_inv = factor_inverse(gram[:half, :half])
    coupled = matmul(upper_inv.T, gram[:half, half:])
    lower_right, lower_inv = factor_inverse(gram[half:, half:] - matmul(coupled.T, coupled))
    zeros_block = jnp.zeros((order - half, half), gram.dtype)
    whole = jnp.concatenate(
        [
            jnp.concatenate([upper_left, coupled], axis=1),
            jnp.concatenate([zeros_block, lower_right], axis=1),
        ],
        axis=0,
    )
    corner = -matmul(matmul(upper_inv, coupled), lower_inv)
    inverse = jnp.concatenate(
        [
            jnp.concatenate([upper_inv, corner], axis=1),
            jnp.concatenate([zeros_block, lower_inv], axis=1),
        ],
        axis=0,
    )
    return (whole, inverse)


def upper_factor(gram):
    return factor_inverse(gram)[0]


def on_device(panel, slab):
    total_rows = panel.shape[0] * lax.axis_size("row")
    scale = 1.0 / total_rows
    contract = (((0,), (0,)), ((), ()))
    local_gram = lax.dot_general(panel, panel, contract, preferred_element_type=jnp.float32) * scale
    local_cross = lax.dot_general(panel, slab, contract, preferred_element_type=jnp.float32) * scale
    factor = upper_factor(lax.psum(local_gram, "row"))
    cross = lax.psum(local_cross, "row")
    inverse = factor_inverse(matmul(factor.T, factor))[1]
    coupling = matmul(inverse.T, cross)
    update = matmul(inverse, coupling).astype(jnp.bfloat16)
    remainder = (
        slab.astype(jnp.float32) - jnp.dot(panel, update, preferred_element_type=jnp.float32)
    ).astype(jnp.bfloat16)
    share = factor.shape[1] // lax.axis_size("col")
    factor_part = lax.dynamic_slice_in_dim(factor, lax.axis_index("col") * share, share, 1)
    return (factor_part, coupling, remainder)


def solution(mesh):
    return jax.shard_map(
        on_device,
        mesh=mesh,
        in_specs=(P("row", None), P("row", "col")),
        out_specs=(P(None, "col"), P(None, "col"), P("row", "col")),
        check_vma=False,
    )
```

profile of v0, /device:TPU:0, one launch (start us, length us, event | category | flops | bytes accessed | tf_op | source)
XLA Modules:
  0.0 1080.7 jit_solution(11859568985775000691)
XLA Ops:
  7.2 1.5 copy-done
  8.8 1.4 convolution_multiply_fusion.1
  10.2 0.8 copy-done.2
  11.0 2.1 convolution_multiply_fusion
  13.1 6.3 copy.270
  19.5 108.3 %all-reduce.377.cloned.1.call-done = (f32[256,256]{1,0:T(8,128)}, f32[256,512]{1,0:T(8,128)}) async-done(((f32[256,256]{1,0:T(8,128)}, f32[256,512]{1,0:T(8,128)}), (f32[256,256]{1,0:T(8,128)}, f32[256,512]{1,0:T(8,128)})) %all-reduce.377.cloned.1.call-update) | async-done | bytes 786448 | tf_op jit(solution)/shard_map/psum | solution.py:49
  127.8 1.5 fusion.2838
  131.4 0.8 fusion.2263
  132.4 0.9 convolution_subtract_fusion.253
  136.3 0.9 fusion.1810
  137.2 0.9 convolution_subtract_fusion.125
  144.9 1.0 fusion.1254
  145.9 0.9 convolution_subtract_fusion.61
  161.0 1.0 fusion.777
  162.0 0.9 convolution_subtract_fusion.29
  191.7 1.0 fusion.450
  192.7 0.9 convolution_subtract_fusion.13
  251.4 1.1 fusion.237
  252.5 1.0 convolution_subtract_fusion.5
  299.0 0.7 fusion.3070
  1061.5 0.7 fusion.2835
  1062.2 0.8 copy-done.5
  1063.7 3.3 fusion
  1067.0 6.4 copy.271
  (1894 shorter events, 407.9 us)
Async XLA Ops:
  7.2 1.6 copy-start
  7.2 120.6 %all-reduce.377.cloned.1.call-start = ((), (), s32[]{:S(2)}) async-start(), calls=%async_computation | async-start | bytes 1572864 | tf_op jit(solution)/shard_map/psum | solution.py:49
  8.8 2.3 copy-start.2
  127.8 240.6 %copy-start.3 = (f32[256,256]{1,0:T(8,128)S(1)}, f32[256,256]{1,0:T(8,128)}, u32[]{:S(2)}) copy-start(f32[256,256]{1,0:T(8,128)} %get-tuple-element.6) | copy-start | bytes 786436
  833.0 228.4 %copy-start.4 = (f32[256,512]{1,0:T(8,128)S(1)}, f32[256,512]{1,0:T(8,128)}, u32[]{:S(2)}) copy-start(f32[256,512]{1,0:T(8,128)} %get-tuple-element.7) | copy-start | bytes 1572868
  1059.8 3.9 copy-start.1
  1062.2 0.8 copy-start.5
Sparse Core Ops, SparseCore 0:
  14.0 113.7 all-reduce.376
where the time goes:
time: 1100 us; the launch traced here: 1080 us
  between operations  528 us (48%)
  matrix products  206 us (19%)
  local copies, waits for them, and re-layouts  198 us (18%)
  waiting for transfers between devices  108 us (10%)
  other arithmetic  40.6 us (4%)
    dot_general x1005, matrix products, matmul(): return jnp.dot(left, right, precision=lax.Precision.HIGHEST)  199 us
    slice x256, local copies, waits for them, and re-layouts, factor_inverse(): coupled = matmul(upper_inv.T, gram[:half, half:])  172 us
    psum x1, waiting for transfers between devices, on_device(): factor = upper_factor(lax.psum(local_gram, 'row'))  108 us
    concatenate x374, other arithmetic, factor_inverse(): jnp.concatenate([jnp.concatenate([upper_inv, corner], axis=1), jnp.concat...  30.4 us
  transfers between devices with their start and end apart: 1, of which 1 were waited for; matrix products, arithmetic and copies ran while one was open for 1% of the time, Pallas kernels for 0%

commit v1 on v0

--- a/solution.py
+++ b/solution.py
@@ -46,7 +46,7 @@
     contract = (((0,), (0,)), ((), ()))
     local_gram = lax.dot_general(panel, panel, contract, preferred_element_type=jnp.float32) * scale
     local_cross = lax.dot_general(panel, slab, contract, preferred_element_type=jnp.float32) * scale
-    factor = upper_factor(lax.psum(local_gram, "row"))
+    factor = upper_factor(jnp.sum(lax.all_gather(local_gram, "row"), axis=0))
     cross = lax.psum(local_cross, "row")
     inverse = factor_inverse(matmul(factor.T, factor))[1]
     coupling = matmul(inverse.T, cross)

time: 1100 us -> 1060 us (0.964)
  waiting for transfers between devices: 108 us -> 68.2 us
    psum x1, waiting for transfers between devices: 108 us -> 0.02 us  [on_device(): cross = lax.psum(local_cross, 'row')]
    all_gather x0 -> x1, waiting for transfers between devices: none -> 68.2 us  [on_device(): factor = upper_factor(jnp.sum(lax.all_gather(local_gram, 'row'), axis=0))]
  transfers between devices with their start and end apart: 1 -> 2, of which waited for: 1 -> 1; matrix products, arithmetic and copies ran while one was open for 1% -> 41% of each run, Pallas kernels for 0% -> 0%
where the time goes in v1:
time: 1060 us; the launch traced here: 1040 us
  between operations  533 us (50%)
  matrix products  200 us (19%)
  local copies, waits for them, and re-layouts  196 us (18%)
  waiting for transfers between devices  68.2 us (6%)
  other arithmetic  43.1 us (4%)
    dot_general x1005, matrix products, matmul(): return jnp.dot(left, right, precision=lax.Precision.HIGHEST)  191 us
    slice x256, local copies, waits for them, and re-layouts, factor_inverse(): coupled = matmul(upper_inv.T, gram[:half, half:])  171 us
    all_gather x1, waiting for transfers between devices, on_device(): factor = upper_factor(jnp.sum(lax.all_gather(local_gram, 'row'), axis=0))  68.2 us
    concatenate x374, other arithmetic, factor_inverse(): jnp.concatenate([jnp.concatenate([upper_inv, corner], axis=1), jnp.concat...  30.4 us
  transfers between devices with their start and end apart: 2, of which 1 were waited for; matrix products, arithmetic and copies ran while one was open for 41% of the time, Pallas kernels for 0%

profile of v1, /device:TPU:0, one launch (start us, length us, event | category | flops | bytes accessed | tf_op | source)
XLA Modules:
  0.0 1040.9 jit_solution(12242282863881807910)
XLA Ops:
  7.2 1.5 copy-done
  8.8 1.5 convolution_multiply_fusion.1
  10.3 4.2 convolution_multiply_fusion
  14.6 6.3 copy.270
  20.9 68.2 %all-gather.3.cloned.1.call-done = f32[4096,256]{1,0:T(8,128)} async-done(((f32[256,256]{1,0:T(8,128)}), f32[4096,256]{1,0:T(8,128)}) %all-gather.3.cloned.1.call-update) | async-done | bytes 4194320 | tf_op jit(solution)/shard_map/all_gather | solution.py:49
  89.1 2.5 reduce_sum.9
  112.3 0.7 fusion.2963
  222.4 0.7 fusion.2896
  237.1 0.7 fusion.2866
  258.0 0.7 fusion.2953
  280.2 0.7 fusion.2894
  294.8 0.7 fusion.2865
  354.1 0.7 fusion.2864
  425.6 0.7 fusion.2889
  469.0 0.7 fusion.2862
  504.1 0.7 fusion.2936
  511.5 0.7 fusion.2886
  580.4 0.7 fusion.3026
  594.8 0.7 fusion.3024
  623.5 0.7 fusion.3020
  680.5 0.7 fusion.3012
  1021.4 1.9 fusion.2835
  1024.0 3.3 fusion
  1027.3 6.4 copy.271
  (1892 shorter events, 401.7 us)
Async XLA Ops:
  7.2 1.6 copy-start
  7.2 81.9 %all-gather.3.cloned.1.call-start = ((), (), s32[]{:S(2)}) async-start(), calls=%async_computation.1 | async-start | bytes 4456448 | tf_op jit(solution)/shard_map/all_gather | solution.py:49
  10.3 1011.1 %all-reduce.376.cloned.1.call-start = ((), (), s32[]{:S(2)}) async-start(), calls=%async_computation | async-start | bytes 1048576 | tf_op jit(solution)/shard_map/psum | solution.py:50
  1021.4 2.6 copy-start.1
  1023.3 4.0 copy-start.2
Sparse Core Ops, SparseCore 0:
  10.8 78.3 all-gather.2
  94.8 108.3 all-reduce.375
